TPU v7x, 32 devices: a whole 2x2x4 slice. The times are simulated.
32 devices in a mesh: groups: 2 (over y), ctx: 16 (over z, x, core).
Axes of the slice: x: 2, y: 2, z: 4, core: 2. Of those that a mesh axis runs over, the one named last changes fastest.
Arguments:
- self_qkv: bfloat16 [3, 8192, 2048], P(None, ('groups', 'ctx')), parts along dimension 1, may hold values from -64 to 64
- windows: int32 [16], replicated, may hold values from 256 to 2048, as said below
- k_gain: float32 [2048], replicated, may hold values from 0.25 to 1.75
- cont_qkv: bfloat16 [3, 256, 2048], P(None, ('groups', 'ctx')), parts along dimension 1, may hold values from -64 to 64
- starts: int32 [32], P('groups'), parts along dimension 0, may hold values from 1 to 4096
Outputs:
- self_out: bfloat16 [8192, 2048], P(('groups', 'ctx')), parts along dimension 0
- cross_out: bfloat16 [256, 2048], P(('groups', 'ctx')), parts along dimension 0
There are 2 independent parts, one for each index of `groups`. A program takes and returns all parts, laid end to end along the dimension named above; an argument that names none is the same for every part. Nothing has to cross between parts.
Inputs may be any that keep to these rules, and one draw needn't show every extreme that they name: `windows`: some head has a window of exactly 2048.
All inputs are finite; a program needn't handle non-finite values.
Results may differ from a plain program's by a relative error of at most 0.0055.
Values may be sent and summed in bfloat16 or wider, within the bound.
No kernel may reach another device: no remote copies, remote signals or barrier semaphores. Data moves between devices by JAX's collectives and lax.ppermute only.
A program may use at most 128 MiB of HBM per device.

v0:
```python
import math
import jax
import jax.numpy as jnp
from jax import lax
from jax.sharding import PartitionSpec as P

WIN = 2048
CLEN = 8
EPSILON = 1e-06
NEGATIVE = -1e30


def shifted(value, axis, steps):
    count = lax.axis_size(axis)
    initial, last = (max(0, -steps), min(count, count - steps))
    return lax.ppermute(value, axis, [(source, source + steps) for source in range(initial, last)])


def finish_rows(cache_high, cache_totals, weighted, own_rows):
    rows_here = own_rows.shape[1]
    features = own_rows.shape[2]
    head_count = cache_high.shape[1]
    head_dim = features // head_count
    groups_here = rows_here // CLEN
    parts = own_rows.reshape(3, groups_here, CLEN, head_count, head_dim)
    scaling = 1.0 / math.sqrt(head_dim)
    scores = (
        jnp.einsum("cihd,cjhd->hcij", parts[0], parts[1], preferred_element_type=jnp.float32)
        * scaling
    )
    causal = (jnp.arange(CLEN)[None, :] <= jnp.arange(CLEN)[:, None])[None, None]
    scores = jnp.where(causal, scores, NEGATIVE)
    prior_high = cache_high.T.reshape(head_count, groups_here, CLEN)
    final = jnp.maximum(prior_high, jnp.max(scores, axis=-1))
    rescale = jnp.exp(prior_high - final)
    expo = jnp.where(causal, jnp.exp(scores - final[..., None]), 0.0)
    totals = rescale * cache_totals.T.reshape(head_count, groups_here, CLEN) + jnp.sum(
        expo, axis=-1
    )
    own_sum = jnp.einsum(
        "hcij,cjhd->cihd", expo.astype(jnp.bfloat16), parts[2], preferred_element_type=jnp.float32
    )
    merged = (
        weighted.reshape(groups_here, CLEN, head_count, head_dim)
        * jnp.transpose(rescale, (1, 2, 0))[..., None]
        + own_sum
    )
    result = merged / jnp.transpose(totals, (1, 2, 0))[..., None]
    return result.reshape(rows_here, features).astype(jnp.bfloat16)


def per_device(self_qkv, windows, k_gain, cont_qkv, starts):
    length = self_qkv.shape[1]
    features = self_qkv.shape[2]
    head_count = windows.shape[0]
    head_dim = features // head_count
    scaling = 1.0 / math.sqrt(head_dim)
    anchor = lax.axis_index("ctx") * length
    reach = WIN // length
    width = (reach + 1) * length
    key_value = self_qkv[1:3]
    earlier = []
    for distance in range(1, reach + 1):
        earlier.append(shifted(key_value, "ctx", distance))
    band = jnp.concatenate(earlier[::-1] + [key_value], axis=1)
    distance_grid = (
        jnp.arange(length, dtype=jnp.int32)[:, None]
        + reach * length
        - jnp.arange(width, dtype=jnp.int32)[None, :]
    )
    key_position = anchor - reach * length + jnp.arange(width, dtype=jnp.int32)

    def one_head(head):
        offset = head * head_dim
        queries = lax.dynamic_slice_in_dim(self_qkv[0], offset, head_dim, 1)
        keys = lax.dynamic_slice_in_dim(band[0], offset, head_dim, 1)
        values = lax.dynamic_slice_in_dim(band[1], offset, head_dim, 1)
        scores = (
            jnp.einsum("id,jd->ij", queries, keys, preferred_element_type=jnp.float32) * scaling
        )
        visible = (
            (distance_grid >= 0) & (distance_grid < windows[head]) & (key_position >= 0)[None, :]
        )
        scores = jnp.where(visible, scores, NEGATIVE)
        highest = jnp.max(scores, axis=-1, keepdims=True)
        expo = jnp.where(visible, jnp.exp(scores - highest), 0.0)
        weights = (expo / jnp.sum(expo, axis=-1, keepdims=True)).astype(jnp.bfloat16)
        return jnp.dot(weights, values, preferred_element_type=jnp.float32).astype(jnp.bfloat16)

    attended = lax.map(one_head, jnp.arange(head_count, dtype=jnp.int32))
    self_out = jnp.transpose(attended, (1, 0, 2)).reshape(length, features)
    hidden = self_out.astype(jnp.float32).reshape(length, head_count, head_dim)
    normed = hidden * lax.rsqrt(jnp.mean(hidden * hidden, axis=-1, keepdims=True) + EPSILON)
    cache_keys = (
        (normed.reshape(length, features) * k_gain)
        .astype(jnp.bfloat16)
        .reshape(length, head_count, head_dim)
    )
    cache_values = self_out.reshape(length, head_count, head_dim)
    gathered = lax.all_gather(cont_qkv[0], "ctx", axis=0, tiled=True)
    rows_all = gathered.shape[0]
    rows_here = cont_qkv.shape[1]
    conts_all = starts.shape[0]
    row_start = jnp.broadcast_to(starts[:, None], (conts_all, rows_all // conts_all)).reshape(
        rows_all
    )
    positions = anchor + jnp.arange(length, dtype=jnp.int32)
    block = math.gcd(rows_all, 512)
    block_count = rows_all // block
    query_blocks = gathered.reshape(block_count, block, head_count, head_dim)
    start_blocks = row_start.reshape(block_count, block)

    def block_scores(query_block, start_block):
        raw = (
            jnp.einsum("ihd,jhd->hij", query_block, cache_keys, preferred_element_type=jnp.float32)
            * scaling
        )
        seen = (positions[None, :] < start_block[:, None])[None]
        return (jnp.where(seen, raw, NEGATIVE), seen)

    def local_part(inputs):
        query_block, start_block = inputs
        masked, seen = block_scores(query_block, start_block)
        peak = jnp.max(masked, axis=-1)
        local_expo = jnp.where(seen, jnp.exp(masked - peak[..., None]), 0.0)
        totals = jnp.sum(local_expo, axis=-1)
        summed = jnp.einsum(
            "hij,jhd->ihd",
            local_expo.astype(jnp.bfloat16),
            cache_values,
            preferred_element_type=jnp.float32,
        )
        return (summed.reshape(block, features), peak.T, totals.T)

    summed, peaks, totals = lax.map(local_part, (query_blocks, start_blocks))
    sources = lax.axis_size("ctx")
    summed = summed.reshape(sources, rows_here, features)
    peaks = peaks.reshape(sources, rows_here, head_count)
    totals = totals.reshape(sources, rows_here, head_count)
    summed_in, peaks_in, totals_in = (
        lax.all_to_all(
            summed.astype(jnp.bfloat16), "ctx", split_axis=0, concat_axis=0, tiled=True
        ).astype(summed.dtype),
        lax.all_to_all(
            peaks.astype(jnp.bfloat16), "ctx", split_axis=0, concat_axis=0, tiled=True
        ).astype(peaks.dtype),
        lax.all_to_all(
            totals.astype(jnp.bfloat16), "ctx", split_axis=0, concat_axis=0, tiled=True
        ).astype(totals.dtype),
    )
    cache_high = jnp.max(peaks_in, axis=0)
    rescale = jnp.exp(peaks_in - cache_high[None])
    weighted = jnp.sum(
        summed_in.reshape(sources, rows_here, head_count, head_dim) * rescale[..., None], axis=0
    )
    cache_totals = jnp.sum(rescale * totals_in, axis=0)
    cross_out = finish_rows(cache_high, cache_totals, weighted, cont_qkv)
    return (self_out, cross_out)


def solution(mesh):
    in_specs = (
        P(None, ("groups", "ctx"), None),
        P(),
        P(),
        P(None, ("groups", "ctx"), None),
        P("groups"),
    )
    out_specs = (P(("groups", "ctx"), None), P(("groups", "ctx"), None))
    return jax.shard_map(
        per_device, mesh=mesh, in_specs=in_specs, out_specs=out_specs, check_vma=False
    )
```

profile of v0, /device:TPU:0, one launch (start us, length us, event | category | flops | bytes accessed | tf_op | source)
XLA Modules:
  0.0 854.6 jit_solution(9346026822741052805)
XLA Ops:
  0.7 3.2 slice.25
  3.9 7.3 collective-permute-start
  11.2 4.9 collective-permute-start.1
  16.1 3.5 collective-permute-start.2
  19.6 2.6 collective-permute-start.3
  23.8 32.4 %collective-permute-done = bf16[2,256,2048]{2,1,0:T(8,128)(2,1)} collective-permute-done((bf16[2,256,2048]{2,1,0:T(8,128)(2,1)}, bf16[2,256,2048]{2,1,0:T(8,128)(2,1)}, u32[]{:S(2)}, u32[]{:S(2)}) %collective-permute-start) | collective-permute-done | bytes 2097184 | tf_op jit(solution)/shard_map/ppermute | solution.py:16
  56.2 2.6 collective-permute-start.5
  59.1 301.0 %all-gather = bf16[1,128,2048]{2,1,0:T(8,128)(2,1)S(1)} all-gather(bf16[1,8,2048]{2,1,0:T(8,128)(2,1)S(1)} %slice-done), channel_id=2, replica_groups=mesh['groups'=2,'ctx'=16] {'ctx'}, dimensions={1}, use_global_device_ids=true | all-gather | bytes 557056 | tf_op jit(solution)/shard_map/all_gather | solution.py:100
  360.0 3.6 collective-permute-start.6
  363.8 3.1 collective-permute-start.7
  376.9 30.9 %collective-permute-done.6 = bf16[2,256,2048]{2,1,0:T(8,128)(2,1)} collective-permute-done((bf16[2,256,2048]{2,1,0:T(8,128)(2,1)}, bf16[2,256,2048]{2,1,0:T(8,128)(2,1)}, u32[]{:S(2)}, u32[]{:S(2)}) %collective-permute-start.6) | collective-permute-done | bytes 2097184 | tf_op jit(solution)/shard_map/ppermute | solution.py:16
  412.3 6.5 copy-done
  418.7 278.3 %while.8 = (s32[]{:T(128)}, bf16[16,256,128]{2,1,0:T(8,128)(2,1)}, s32[16]{0:T(128)S(1)}, s32[16]{0:T(128)S(1)}, bf16[3,256,2048]{2,1,0:T(8,128)(2,1)S(1)}, /*in...) while((s32[]{:T(128)}, bf16[16,256,128]{2,1,0:T(8,128)(2,1)}, ...), condition=%wide.region_3.4_spmd.clone.clone, body=%wide.region_0.3_spmd.clone.clone.sunk | while | flops 316772352 | bytes 48255728 | solution.py:90
  422.0 8.1 fusion.75
  433.6 2.5 fusion.78
  439.4 8.1 fusion.75
  451.0 2.5 fusion.78
  456.8 8.1 fusion.75
  468.4 2.5 fusion.78
  474.2 8.1 fusion.75
  485.8 2.5 fusion.78
  491.6 8.1 fusion.75
  503.2 2.5 fusion.78
  509.0 8.1 fusion.75
  520.6 2.5 fusion.78
  526.4 8.1 fusion.75
  543.8 8.1 fusion.75
  561.2 8.1 fusion.75
  572.8 2.5 fusion.78
  578.6 8.1 fusion.75
  590.2 2.5 fusion.78
  595.9 8.1 fusion.75
  607.5 2.5 fusion.78
  613.3 8.1 fusion.75
  624.9 2.5 fusion.78
  630.8 8.1 fusion.75
  642.4 2.5 fusion.78
  648.1 8.1 fusion.75
  659.7 2.5 fusion.78
  665.5 8.1 fusion.75
  677.1 2.5 fusion.78
  682.9 8.1 fusion.75
  702.3 116.6 %all-to-all-start.2 = ((bf16[16,8,16]{2,1,0:T(8,128)(2,1)}), bf16[16,8,16]{2,1,0:T(8,128)(2,1)S(1)}, u32[]{:S(2)}, u32[]{:S(2)}) async-start(bf16[16,8,16]{2,1,0:T(8,128)(2,1)} %bitcast.20), calls=%async_computation.2 | async-start | bytes 65536 | tf_op jit(solution)/shard_map/all_to_all | solution.py:147
  819.7 5.9 all-to-all-done.2
  825.6 3.5 all-to-all-start.1
  832.6 3.1 all-to-all-done.1
  835.7 3.6 all-to-all-start
  842.2 11.3 %all-to-all-done = bf16[16,8,2048]{2,1,0:T(8,128)(2,1)S(1)} async-done(((bf16[16,8,2048]{2,1,0:T(8,128)(2,1)}), bf16[16,8,2048]{2,1,0:T(8,128)(2,1)S(1)}, u32[]{:S(2)}, u32[]{:S(2)}) %all-to-all-start) | async-done | bytes 524320 | tf_op jit(solution)/shard_map/all_to_all | solution.py:141
  (163 shorter events, 110.5 us)
Async XLA Ops:
  0.6 23.0 %copy-start.2 = (bf16[3,8,2048]{2,1,0:T(8,128)(2,1)S(1)}, bf16[3,8,2048]{2,1,0:T(8,128)(2,1)}, u32[]{:S(2)}) copy-start(bf16[3,8,2048]{2,1,0:T(8,128)(2,1)} %param.10) | copy-start | bytes 294916
  0.6 58.4 %slice-start = ((bf16[3,8,2048]{2,1,0:T(8,128)(2,1)}), bf16[1,8,2048]{2,1,0:T(8,128)(2,1)S(1)}, s32[]{:S(2)}) async-start(bf16[3,8,2048]{2,1,0:T(8,128)(2,1)} %param.10), calls=%async_computation.3 | async-start | bytes 65536 | tf_op jit(solution)/shard_map/slice | solution.py:100
  0.7 58.2 %copy-start.3 = (s32[16]{0:T(128)S(1)}, s32[16]{0:T(128)}, u32[]{:S(2)}) copy-start(s32[16]{0:T(128)} %param.11) | copy-start | bytes 196
  3.9 52.3 %collective-permute-start = (bf16[2,256,2048]{2,1,0:T(8,128)(2,1)}, bf16[2,256,2048]{2,1,0:T(8,128)(2,1)}, u32[]{:S(2)}, u32[]{:S(2)}) collective-permute-start(bf16[2,256,2048]{2,1,0:T(8,128)(2,1)} %slice.25), channel_id=1, source_target_pairs={{0,8},{1,9},{2,10},{3,11},{4,12},{5,13},{6,14},{7,15},{16,24},{17,... | collective-permute-start | bytes 6291464 | tf_op jit(solution)/shard_map/ppermute | solution.py:16
  11.2 348.9 %collective-permute-start.1 = (bf16[2,256,2048]{2,1,0:T(8,128)(2,1)}, bf16[2,256,2048]{2,1,0:T(8,128)(2,1)}, u32[]{:S(2)}, u32[]{:S(2)}) collective-permute-start(bf16[2,256,2048]{2,1,0:T(8,128)(2,1)} %slice.25), channel_id=1, source_target_pairs={{0,7},{1,8},{2,9},{3,10},{4,11},{5,12},{6,13},{7,14},{8,15},{16,23... | collective-permute-start | bytes 6291464 | tf_op jit(solution)/shard_map/ppermute | solution.py:16
  16.1 347.7 %collective-permute-start.2 = (bf16[2,256,2048]{2,1,0:T(8,128)(2,1)}, bf16[2,256,2048]{2,1,0:T(8,128)(2,1)}, u32[]{:S(2)}, u32[]{:S(2)}) collective-permute-start(bf16[2,256,2048]{2,1,0:T(8,128)(2,1)} %slice.25), channel_id=1, source_target_pairs={{0,6},{1,7},{2,8},{3,9},{4,10},{5,11},{6,12},{7,13},{8,14},{9,15},... | collective-permute-start | bytes 6291464 | tf_op jit(solution)/shard_map/ppermute | solution.py:16
  19.6 353.7 %collective-permute-start.3 = (bf16[2,256,2048]{2,1,0:T(8,128)(2,1)}, bf16[2,256,2048]{2,1,0:T(8,128)(2,1)}, u32[]{:S(2)}, u32[]{:S(2)}) collective-permute-start(bf16[2,256,2048]{2,1,0:T(8,128)(2,1)} %slice.25), channel_id=1, source_target_pairs={{0,5},{1,6},{2,7},{3,8},{4,9},{5,10},{6,11},{7,12},{8,13},{9,14},{... | collective-permute-start | bytes 6291464 | tf_op jit(solution)/shard_map/ppermute | solution.py:16
  22.2 352.8 %collective-permute-start.4 = (bf16[2,256,2048]{2,1,0:T(8,128)(2,1)}, bf16[2,256,2048]{2,1,0:T(8,128)(2,1)S(1)}, u32[]{:S(2)}, u32[]{:S(2)}) collective-permute-start(bf16[2,256,2048]{2,1,0:T(8,128)(2,1)} %slice.25), channel_id=1, source_target_pairs={{0,4},{1,5},{2,6},{3,7},{4,8},{5,9},{6,10},{7,11},{8,12},{9,13},{1... | collective-permute-start | bytes 6291464 | tf_op jit(solution)/shard_map/ppermute | solution.py:16
  56.2 319.0 %collective-permute-start.5 = (bf16[2,256,2048]{2,1,0:T(8,128)(2,1)}, bf16[2,256,2048]{2,1,0:T(8,128)(2,1)}, u32[]{:S(2)}, u32[]{:S(2)}) collective-permute-start(bf16[2,256,2048]{2,1,0:T(8,128)(2,1)} %slice.25), channel_id=1, source_target_pairs={{0,3},{1,4},{2,5},{3,6},{4,7},{5,8},{6,9},{7,10},{8,11},{9,12},{10... | collective-permute-start | bytes 6291464 | tf_op jit(solution)/shard_map/ppermute | solution.py:16
  360.0 47.8 %collective-permute-start.6 = (bf16[2,256,2048]{2,1,0:T(8,128)(2,1)}, bf16[2,256,2048]{2,1,0:T(8,128)(2,1)}, u32[]{:S(2)}, u32[]{:S(2)}) collective-permute-start(bf16[2,256,2048]{2,1,0:T(8,128)(2,1)} %slice.25), channel_id=1, source_target_pairs={{0,2},{1,3},{2,4},{3,5},{4,6},{5,7},{6,8},{7,9},{8,10},{9,11},{10,... | collective-permute-start | bytes 6291464 | tf_op jit(solution)/shard_map/ppermute | solution.py:16
  363.8 45.8 %collective-permute-start.7 = (bf16[2,256,2048]{2,1,0:T(8,128)(2,1)}, bf16[2,256,2048]{2,1,0:T(8,128)(2,1)}, u32[]{:S(2)}, u32[]{:S(2)}) collective-permute-start(bf16[2,256,2048]{2,1,0:T(8,128)(2,1)} %slice.25), channel_id=1, source_target_pairs={{0,1},{1,2},{2,3},{3,4},{4,5},{5,6},{6,7},{7,8},{8,9},{9,10},{10,1... | collective-permute-start | bytes 6291464 | tf_op jit(solution)/shard_map/ppermute | solution.py:16
  409.6 2.5 copy-start.1
  412.1 6.6 copy-start.5
  412.3 6.5 copy-start
  418.7 280.1 %copy-start.4 = (f32[2048]{0:T(1024)S(1)}, f32[2048]{0:T(1024)}, u32[]{:S(2)}) copy-start(f32[2048]{0:T(1024)} %param.9) | copy-start | bytes 24580
  702.3 123.3 %all-to-all-start.2 = ((bf16[16,8,16]{2,1,0:T(8,128)(2,1)}), bf16[16,8,16]{2,1,0:T(8,128)(2,1)S(1)}, u32[]{:S(2)}, u32[]{:S(2)}) async-start(bf16[16,8,16]{2,1,0:T(8,128)(2,1)} %bitcast.20), calls=%async_computation.2 | async-start | bytes 65536 | tf_op jit(solution)/shard_map/all_to_all | solution.py:147
  825.6 10.1 %all-to-all-start.1 = ((bf16[16,8,16]{2,1,0:T(8,128)(2,1)}), bf16[16,8,16]{2,1,0:T(8,128)(2,1)S(1)}, u32[]{:S(2)}, u32[]{:S(2)}) async-start(bf16[16,8,16]{2,1,0:T(8,128)(2,1)} %bitcast.6), calls=%async_computation.1 | async-start | bytes 65536 | tf_op jit(solution)/shard_map/all_to_all | solution.py:144
  835.7 17.8 %all-to-all-start = ((bf16[16,8,2048]{2,1,0:T(8,128)(2,1)}), bf16[16,8,2048]{2,1,0:T(8,128)(2,1)S(1)}, u32[]{:S(2)}, u32[]{:S(2)}) async-start(bf16[16,8,2048]{2,1,0:T(8,128)(2,1)} %convert_element_type.69), calls=%async_computation | async-start | bytes 1048576 | tf_op jit(solution)/shard_map/all_to_all | solution.py:141
where the time goes:
time: 856 us; the launch traced here: 855 us
  blocking collectives  301 us (35%)
  local copies, waits for them, and re-layouts  179 us (21%)
  starting transfers between devices  153 us (18%)
  waiting for transfers between devices  83.7 us (10%)
  matrix products  71.8 us (8%)
  loops' own time  35.4 us (4%)
  other arithmetic  30.3 us (4%)
    all_gather x1, blocking collectives, per_device(): gathered = lax.all_gather(cont_qkv[0], 'ctx', axis=0, tiled=True)  301 us
    slice x16, local copies, waits for them, and re-layouts, one_head(): values = lax.dynamic_slice_in_dim(band[1], offset, head_dim, 1)  130 us
    all_to_all x1, starting transfers between devices, per_device(): lax.all_to_all(totals.astype(jnp.bfloat16), 'ctx', split_axis=0, concat_a...  117 us
    ppermute x8, waiting for transfers between devices, shifted(): lax.ppermute(value, axis, [(source, source + steps) for source in range(i...  63.4 us
    dot_general x16, matrix products, one_head(): jnp.dot(weights, values, preferred_element_type=jnp.float32)  39.7 us
    another operation x1, loops' own time, per_device(): attended = lax.map(one_head, jnp.arange(head_count, dtype=jnp.int32))  35.4 us
    ppermute x8, starting transfers between devices, shifted(): lax.ppermute(value, axis, [(source, source + steps) for source in range(i...  29.1 us
    reduce_sum x16, other arithmetic, one_head(): jnp.sum(expo, axis=-1, keepdims=True)  27.1 us
  transfers between devices with their start and end apart: 11, of which 5 were waited for; matrix products, arithmetic and copies ran while one was open for 2% of the time, Pallas kernels for 0%

commit v1 on v0

--- a/solution.py
+++ b/solution.py
@@ -8,6 +8,23 @@
 CLEN = 8
 EPSILON = 1e-06
 NEGATIVE = -1e30
+
+
+def joined_along(tiles, dim):
+    shape = list(tiles.shape[1:])
+    shape[dim] *= tiles.shape[0]
+    return jnp.moveaxis(tiles, 0, dim).reshape(shape)
+
+
+def gather_around(value, axis, dim):
+    devices = lax.axis_size(axis)
+    right = [(i, (i + 1) % devices) for i in range(devices)]
+    parts = [value]
+    while len(parts) < devices:
+        parts.append(lax.ppermute(parts[-1], axis, right))
+    index = lax.axis_index(axis)
+    parts = jnp.stack(parts)[(index - jnp.arange(devices)) % devices]
+    return joined_along(parts, dim)
 
 
 def shifted(value, axis, steps):
@@ -97,7 +114,7 @@
         .reshape(length, head_count, head_dim)
     )
     cache_values = self_out.reshape(length, head_count, head_dim)
-    gathered = lax.all_gather(cont_qkv[0], "ctx", axis=0, tiled=True)
+    gathered = gather_around(cont_qkv[0], "ctx", 0)
     rows_all = gathered.shape[0]
     rows_here = cont_qkv.shape[1]
     conts_all = starts.shape[0]

time: 856 us -> 913 us (1.067)
  blocking collectives: 301 us -> 0 us
  starting transfers between devices: 153 us -> 395 us
  waiting for transfers between devices: 83.7 us -> 186 us
    all_gather x1 -> x0, blocking collectives: 301 us -> none  [per_device(): gathered = lax.all_gather(cont_qkv[0], 'ctx', axis=0, tiled=True)]
    ppermute x0 -> x15, starting transfers between devices: none -> 284 us  [gather_around(): parts.append(lax.ppermute(parts[-1], axis, right))]
    ppermute x0 -> x15, waiting for transfers between devices: none -> 96 us  [gather_around(): parts.append(lax.ppermute(parts[-1], axis, right))]
    all_to_all x1, starting transfers between devices: 117 us -> 65.7 us  [per_device(): lax.all_to_all(totals.astype(jnp.bfloat16), 'ctx', split_axis=0, concat_a...]
    unnamed x20 -> x35, local copies, waits for them, and re-layouts: 19.5 us -> 20.4 us
  transfers between devices with their start and end apart: 11 -> 26, of which waited for: 5 -> 21; matrix products, arithmetic and copies ran while one was open for 2% -> 2% of each run, Pallas kernels for 0% -> 0%
where the time goes in v1:
time: 913 us; the launch traced here: 911 us
  starting transfers between devices  395 us (43%)
  waiting for transfers between devices  186 us (20%)
  local copies, waits for them, and re-layouts  181 us (20%)
  matrix products  75 us (8%)
  loops' own time  40.9 us (4%)
  other arithmetic  32 us (4%)
    ppermute x15, starting transfers between devices, gather_around(): parts.append(lax.ppermute(parts[-1], axis, right))  284 us
    slice x16, local copies, waits for them, and re-layouts, one_head(): values = lax.dynamic_slice_in_dim(band[1], offset, head_dim, 1)  130 us
    ppermute x15, waiting for transfers between devices, gather_around(): parts.append(lax.ppermute(parts[-1], axis, right))  96 us
    ppermute x8, waiting for transfers between devices, shifted(): lax.ppermute(value, axis, [(source, source + steps) for source in range(i...  69.6 us
    all_to_all x1, starting transfers between devices, per_device(): lax.all_to_all(totals.astype(jnp.bfloat16), 'ctx', split_axis=0, concat_a...  65.7 us
    dot_general x16, matrix products, one_head(): jnp.dot(weights, values, preferred_element_type=jnp.float32)  41.1 us
    another operation x1, loops' own time, per_device(): attended = lax.map(one_head, jnp.arange(head_count, dtype=jnp.int32))  40.9 us
    ppermute x8, starting transfers between devices, shifted(): lax.ppermute(value, axis, [(source, source + steps) for source in range(i...  37.9 us
  transfers between devices with their start and end apart: 26, of which 21 were waited for; matrix products, arithmetic and copies ran while one was open for 2% of the time, Pallas kernels for 0%

profile of v1, /device:TPU:0, one launch (start us, length us, event | category | flops | bytes accessed | tf_op | source)
XLA Modules:
  0.0 910.6 jit_solution(17302333162454964007)
XLA Ops:
  0.6 3.2 slice.25
  3.9 6.1 collective-permute-start
  10.0 4.9 collective-permute-start.1
  14.8 3.5 collective-permute-start.2
  21.6 5.4 collective-permute-done.8
  27.0 6.0 collective-permute-done.9
  33.1 31.3 %collective-permute-done.10 = bf16[8,2048]{1,0:T(8,128)(2,1)S(1)} collective-permute-done((bf16[8,2048]{1,0:T(8,128)(2,1)S(1)}, bf16[8,2048]{1,0:T(8,128)(2,1)S(1)}, u32[]{:S(2)}, u32[]{:S(2)}) %collective-permute-start.10) | collective-permute-done | bytes 32800 | tf_op jit(solution)/shard_map/ppermute | solution.py:24
  64.4 128.5 %collective-permute-start.11 = (bf16[8,2048]{1,0:T(8,128)(2,1)S(1)}, bf16[8,2048]{1,0:T(8,128)(2,1)S(1)}, u32[]{:S(2)}, u32[]{:S(2)}) collective-permute-start(bf16[8,2048]{1,0:T(8,128)(2,1)S(1)} %collective-permute-done.10), channel_id=1, source_target_pairs={{0,1},{1,2},{2,3},{3,4},{4,5},{5,6},{6,7},{7,8},{8,9},{9,10},{10,1... | collective-permute-start | bytes 98312 | tf_op jit(solution)/shard_map/ppermute | solution.py:24
  193.8 3.5 collective-permute-start.12
  201.6 4.3 collective-permute-done.13
  205.9 6.0 collective-permute-done.14
  211.9 146.0 %collective-permute-start.15 = (bf16[8,2048]{1,0:T(8,128)(2,1)S(1)}, bf16[8,2048]{1,0:T(8,128)(2,1)S(1)}, u32[]{:S(2)}, u32[]{:S(2)}) collective-permute-start(bf16[8,2048]{1,0:T(8,128)(2,1)S(1)} %collective-permute-done.14), channel_id=1, source_target_pairs={{0,1},{1,2},{2,3},{3,4},{4,5},{5,6},{6,7},{7,8},{8,9},{9,10},{10,1... | collective-permute-start | bytes 98312 | tf_op jit(solution)/shard_map/ppermute | solution.py:24
  358.8 3.5 collective-permute-start.16
  362.3 3.4 collective-permute-done.16
  366.6 5.2 collective-permute-done.17
  371.8 6.0 collective-permute-done.18
  377.8 6.0 collective-permute-done.19
  383.8 6.0 collective-permute-done.20
  389.9 6.0 collective-permute-done.21
  395.9 6.0 collective-permute-done.22
  404.6 11.2 %collective-permute-start.5 = (bf16[2,256,2048]{2,1,0:T(8,128)(2,1)}, bf16[2,256,2048]{2,1,0:T(8,128)(2,1)}, u32[]{:S(2)}, u32[]{:S(2)}) collective-permute-start(bf16[2,256,2048]{2,1,0:T(8,128)(2,1)} %slice.25), channel_id=1, source_target_pairs={{0,3},{1,4},{2,5},{3,6},{4,7},{5,8},{6,9},{7,10},{8,11},{9,12},{10... | collective-permute-start | bytes 6291464 | tf_op jit(solution)/shard_map/ppermute | solution.py:33
  418.4 4.4 collective-permute-start.7
  429.6 18.8 %collective-permute-done.4 = bf16[2,256,2048]{2,1,0:T(8,128)(2,1)} collective-permute-done((bf16[2,256,2048]{2,1,0:T(8,128)(2,1)}, bf16[2,256,2048]{2,1,0:T(8,128)(2,1)}, u32[]{:S(2)}, u32[]{:S(2)}) %collective-permute-start.4) | collective-permute-done | bytes 2097184 | tf_op jit(solution)/shard_map/ppermute | solution.py:33
  450.1 7.6 collective-permute-done.5
  459.4 43.2 %collective-permute-done.6 = bf16[2,256,2048]{2,1,0:T(8,128)(2,1)} collective-permute-done((bf16[2,256,2048]{2,1,0:T(8,128)(2,1)}, bf16[2,256,2048]{2,1,0:T(8,128)(2,1)}, u32[]{:S(2)}, u32[]{:S(2)}) %collective-permute-start.6) | collective-permute-done | bytes 2097184 | tf_op jit(solution)/shard_map/ppermute | solution.py:33
  507.0 6.4 copy-done
  513.5 289.6 %while.8 = (s32[]{:T(128)}, bf16[16,256,128]{2,1,0:T(8,128)(2,1)}, s32[16]{0:T(128)S(1)}, s32[16]{0:T(128)S(1)}, bf16[3,256,2048]{2,1,0:T(8,128)(2,1)S(1)}, /*in...) while((s32[]{:T(128)}, bf16[16,256,128]{2,1,0:T(8,128)(2,1)}, ...), condition=%wide.region_3.4_spmd.clone.clone, body=%wide.region_0.3_spmd.clone.clone.sunk | while | flops 316772352 | bytes 48255728 | solution.py:107
  517.2 8.1 fusion.77
  535.3 8.1 fusion.77
  553.4 8.1 fusion.77
  571.6 8.1 fusion.77
  589.7 8.1 fusion.77
  607.8 8.1 fusion.77
  625.9 8.1 fusion.77
  644.0 8.1 fusion.77
  662.1 8.1 fusion.77
  680.2 8.1 fusion.77
  698.3 8.1 fusion.77
  716.4 8.1 fusion.77
  734.5 8.1 fusion.77
  752.6 8.1 fusion.77
  770.7 8.1 fusion.77
  788.8 8.1 fusion.77
  809.2 65.7 %all-to-all-start.2 = ((bf16[16,8,16]{2,1,0:T(8,128)(2,1)}), bf16[16,8,16]{2,1,0:T(8,128)(2,1)S(1)}, u32[]{:S(2)}, u32[]{:S(2)}) async-start(bf16[16,8,16]{2,1,0:T(8,128)(2,1)} %bitcast.35), calls=%async_computation.2 | async-start | bytes 65536 | tf_op jit(solution)/shard_map/all_to_all | solution.py:164
  875.7 5.9 all-to-all-done.2
  881.6 3.7 all-to-all-start.1
  891.7 3.6 all-to-all-start
  898.2 11.3 %all-to-all-done = bf16[16,8,2048]{2,1,0:T(8,128)(2,1)S(1)} async-done(((bf16[16,8,2048]{2,1,0:T(8,128)(2,1)}), bf16[16,8,2048]{2,1,0:T(8,128)(2,1)S(1)}, u32[]{:S(2)}, u32[]{:S(2)}) %all-to-all-start) | async-done | bytes 524320 | tf_op jit(solution)/shard_map/all_to_all | solution.py:158
  (209 shorter events, 166.1 us)
Async XLA Ops:
  0.6 20.3 %copy-start.2 = (bf16[3,8,2048]{2,1,0:T(8,128)(2,1)S(1)}, bf16[3,8,2048]{2,1,0:T(8,128)(2,1)}, u32[]{:S(2)}) copy-start(bf16[3,8,2048]{2,1,0:T(8,128)(2,1)} %param.10) | copy-start | bytes 294916
  0.6 20.5 %copy-start.3 = (s32[16]{0:T(128)S(1)}, s32[16]{0:T(128)}, u32[]{:S(2)}) copy-start(s32[16]{0:T(128)} %param.11) | copy-start | bytes 196
  3.9 400.7 %collective-permute-start = (bf16[2,256,2048]{2,1,0:T(8,128)(2,1)}, bf16[2,256,2048]{2,1,0:T(8,128)(2,1)S(1)}, u32[]{:S(2)}, u32[]{:S(2)}) collective-permute-start(bf16[2,256,2048]{2,1,0:T(8,128)(2,1)} %slice.25), channel_id=1, source_target_pairs={{0,8},{1,9},{2,10},{3,11},{4,12},{5,13},{6,14},{7,15},{16,24},{17,... | collective-permute-start | bytes 6291464 | tf_op jit(solution)/shard_map/ppermute | solution.py:33
  10.0 405.8 %collective-permute-start.1 = (bf16[2,256,2048]{2,1,0:T(8,128)(2,1)}, bf16[2,256,2048]{2,1,0:T(8,128)(2,1)}, u32[]{:S(2)}, u32[]{:S(2)}) collective-permute-start(bf16[2,256,2048]{2,1,0:T(8,128)(2,1)} %slice.25), channel_id=1, source_target_pairs={{0,7},{1,8},{2,9},{3,10},{4,11},{5,12},{6,13},{7,14},{8,15},{16,23... | collective-permute-start | bytes 6291464 | tf_op jit(solution)/shard_map/ppermute | solution.py:33
  14.8 403.5 %collective-permute-start.2 = (bf16[2,256,2048]{2,1,0:T(8,128)(2,1)}, bf16[2,256,2048]{2,1,0:T(8,128)(2,1)}, u32[]{:S(2)}, u32[]{:S(2)}) collective-permute-start(bf16[2,256,2048]{2,1,0:T(8,128)(2,1)} %slice.25), channel_id=1, source_target_pairs={{0,6},{1,7},{2,8},{3,9},{4,10},{5,11},{6,12},{7,13},{8,14},{9,15},... | collective-permute-start | bytes 6291464 | tf_op jit(solution)/shard_map/ppermute | solution.py:33
  18.3 409.5 %collective-permute-start.3 = (bf16[2,256,2048]{2,1,0:T(8,128)(2,1)}, bf16[2,256,2048]{2,1,0:T(8,128)(2,1)}, u32[]{:S(2)}, u32[]{:S(2)}) collective-permute-start(bf16[2,256,2048]{2,1,0:T(8,128)(2,1)} %slice.25), channel_id=1, source_target_pairs={{0,5},{1,6},{2,7},{3,8},{4,9},{5,10},{6,11},{7,12},{8,13},{9,14},{... | collective-permute-start | bytes 6291464 | tf_op jit(solution)/shard_map/ppermute | solution.py:33
  20.9 6.1 collective-permute-start.8
  27.0 6.0 collective-permute-start.9
  33.1 31.3 %collective-permute-start.10 = (bf16[8,2048]{1,0:T(8,128)(2,1)S(1)}, bf16[8,2048]{1,0:T(8,128)(2,1)S(1)}, u32[]{:S(2)}, u32[]{:S(2)}) collective-permute-start(bf16[8,2048]{1,0:T(8,128)(2,1)S(1)} %collective-permute-done.9), channel_id=1, source_target_pairs={{0,1},{1,2},{2,3},{3,4},{4,5},{5,6},{6,7},{7,8},{8,9},{9,10},{10,1... | collective-permute-start | bytes 98312 | tf_op jit(solution)/shard_map/ppermute | solution.py:24
  64.4 129.4 %collective-permute-start.11 = (bf16[8,2048]{1,0:T(8,128)(2,1)S(1)}, bf16[8,2048]{1,0:T(8,128)(2,1)S(1)}, u32[]{:S(2)}, u32[]{:S(2)}) collective-permute-start(bf16[8,2048]{1,0:T(8,128)(2,1)S(1)} %collective-permute-done.10), channel_id=1, source_target_pairs={{0,1},{1,2},{2,3},{3,4},{4,5},{5,6},{6,7},{7,8},{8,9},{9,10},{10,1... | collective-permute-start | bytes 98312 | tf_op jit(solution)/shard_map/ppermute | solution.py:24
  193.8 6.0 collective-permute-start.12
  199.8 6.0 collective-permute-start.13
  205.9 6.0 collective-permute-start.14
  211.9 146.9 %collective-permute-start.15 = (bf16[8,2048]{1,0:T(8,128)(2,1)S(1)}, bf16[8,2048]{1,0:T(8,128)(2,1)S(1)}, u32[]{:S(2)}, u32[]{:S(2)}) collective-permute-start(bf16[8,2048]{1,0:T(8,128)(2,1)S(1)} %collective-permute-done.14), channel_id=1, source_target_pairs={{0,1},{1,2},{2,3},{3,4},{4,5},{5,6},{6,7},{7,8},{8,9},{9,10},{10,1... | collective-permute-start | bytes 98312 | tf_op jit(solution)/shard_map/ppermute | solution.py:24
  358.8 7.0 collective-permute-start.16
  365.7 6.0 collective-permute-start.17
  371.8 6.0 collective-permute-start.18
  377.8 6.0 collective-permute-start.19
  383.8 6.0 collective-permute-start.20
  389.9 6.0 collective-permute-start.21
  395.9 6.0 collective-permute-start.22
  401.9 46.4 %collective-permute-start.4 = (bf16[2,256,2048]{2,1,0:T(8,128)(2,1)}, bf16[2,256,2048]{2,1,0:T(8,128)(2,1)}, u32[]{:S(2)}, u32[]{:S(2)}) collective-permute-start(bf16[2,256,2048]{2,1,0:T(8,128)(2,1)} %slice.25), channel_id=1, source_target_pairs={{0,4},{1,5},{2,6},{3,7},{4,8},{5,9},{6,10},{7,11},{8,12},{9,13},{1... | collective-permute-start | bytes 6291464 | tf_op jit(solution)/shard_map/ppermute | solution.py:33
  404.6 53.1 %collective-permute-start.5 = (bf16[2,256,2048]{2,1,0:T(8,128)(2,1)}, bf16[2,256,2048]{2,1,0:T(8,128)(2,1)}, u32[]{:S(2)}, u32[]{:S(2)}) collective-permute-start(bf16[2,256,2048]{2,1,0:T(8,128)(2,1)} %slice.25), channel_id=1, source_target_pairs={{0,3},{1,4},{2,5},{3,6},{4,7},{5,8},{6,9},{7,10},{8,11},{9,12},{10... | collective-permute-start | bytes 6291464 | tf_op jit(solution)/shard_map/ppermute | solution.py:33
  415.8 86.9 %collective-permute-start.6 = (bf16[2,256,2048]{2,1,0:T(8,128)(2,1)}, bf16[2,256,2048]{2,1,0:T(8,128)(2,1)}, u32[]{:S(2)}, u32[]{:S(2)}) collective-permute-start(bf16[2,256,2048]{2,1,0:T(8,128)(2,1)} %slice.25), channel_id=1, source_target_pairs={{0,2},{1,3},{2,4},{3,5},{4,6},{5,7},{6,8},{7,9},{8,10},{9,11},{10,... | collective-permute-start | bytes 6291464 | tf_op jit(solution)/shard_map/ppermute | solution.py:33
  418.4 86.0 %collective-permute-start.7 = (bf16[2,256,2048]{2,1,0:T(8,128)(2,1)}, bf16[2,256,2048]{2,1,0:T(8,128)(2,1)}, u32[]{:S(2)}, u32[]{:S(2)}) collective-permute-start(bf16[2,256,2048]{2,1,0:T(8,128)(2,1)} %slice.25), channel_id=1, source_target_pairs={{0,1},{1,2},{2,3},{3,4},{4,5},{5,6},{6,7},{7,8},{8,9},{9,10},{10,1... | collective-permute-start | bytes 6291464 | tf_op jit(solution)/shard_map/ppermute | solution.py:33
  504.4 2.5 copy-start.1
  506.9 6.6 copy-start.5
  507.0 6.5 copy-start
  513.5 291.5 %copy-start.4 = (f32[2048]{0:T(1024)S(1)}, f32[2048]{0:T(1024)}, u32[]{:S(2)}) copy-start(f32[2048]{0:T(1024)} %param.9) | copy-start | bytes 24580
  809.2 72.4 %all-to-all-start.2 = ((bf16[16,8,16]{2,1,0:T(8,128)(2,1)}), bf16[16,8,16]{2,1,0:T(8,128)(2,1)S(1)}, u32[]{:S(2)}, u32[]{:S(2)}) async-start(bf16[16,8,16]{2,1,0:T(8,128)(2,1)} %bitcast.35), calls=%async_computation.2 | async-start | bytes 65536 | tf_op jit(solution)/shard_map/all_to_all | solution.py:164
  881.6 10.1 %all-to-all-start.1 = ((bf16[16,8,16]{2,1,0:T(8,128)(2,1)}), bf16[16,8,16]{2,1,0:T(8,128)(2,1)S(1)}, u32[]{:S(2)}, u32[]{:S(2)}) async-start(bf16[16,8,16]{2,1,0:T(8,128)(2,1)} %bitcast.21), calls=%async_computation.1 | async-start | bytes 65536 | tf_op jit(solution)/shard_map/all_to_all | solution.py:161
  891.7 17.8 %all-to-all-start = ((bf16[16,8,2048]{2,1,0:T(8,128)(2,1)}), bf16[16,8,2048]{2,1,0:T(8,128)(2,1)S(1)}, u32[]{:S(2)}, u32[]{:S(2)}) async-start(bf16[16,8,2048]{2,1,0:T(8,128)(2,1)} %convert_element_type.69), calls=%async_computation | async-start | bytes 1048576 | tf_op jit(solution)/shard_map/all_to_all | solution.py:158
